TPU v7x, 512 devices: a whole 4x4x16 slice. The times are simulated.
512 devices in a mesh: rep: 8 (over y, core), exp: 64 (over x, z).
Axes of the slice: x: 4, y: 4, z: 16, core: 2. Of those that a mesh axis runs over, the one named last changes fastest.
Arguments:
- payload: bfloat16 [16384, 2048], P(('rep', 'exp')), may hold values from -6 to 6
- block_scales: bfloat16 [16384, 16], P(('rep', 'exp')), may hold values from 0.29882812 to 3
- cotangent: bfloat16 [16384, 2048], P(('rep', 'exp')), may hold values from -12 to 12
- expert_ids: int32 [16384, 8], P(('rep', 'exp')), may hold values from 0 to 63, all different within a row; in each aligned block of 32 rows (0 to 31, 32 to 63, ...) at most 5 rows name the same one
- route_counts: int32 [16384, 8], P(('rep', 'exp')), may hold values from 1 to 15
- gate_up: bfloat16 [64, 2, 2048, 384], P('exp', None, 'rep'), may hold values from -0.125 to 0.125
- down_weight: bfloat16 [64, 384, 2048], P('exp', None, 'rep'), may hold values from -0.3125 to 0.3125
- first_moment: float32 [64, 2, 2048, 384], P('exp', None, 'rep'), may hold values from -12 to 12
- second_moment: float32 [64, 2, 2048, 384], P('exp', None, 'rep'), may hold values from 10 to 300
Outputs:
- d_activation: bfloat16 [16384, 2048], P(('rep', 'exp'))
- new_first: float32 [64, 2, 2048, 384], P('exp', None, 'rep')
- new_second: float32 [64, 2, 2048, 384], P('exp', None, 'rep')
- weight_step: bfloat16 [64, 2, 2048, 384], P('exp', None, 'rep')
Inputs may be any that keep to these rules, and one draw needn't show every extreme that they name: `expert_ids`: in the rows of one device (aligned blocks of 32 tokens) no expert is named more than 5 times, a bound that some block reaches; each token names 8 different experts.
All inputs are finite; a program needn't handle non-finite values.
Results may differ from a plain program's by a relative error of at most 0.02.
Values may be sent and summed in bfloat16 or wider, within the bound.
A program may use at most 64 MiB of HBM per device.

v0:
```python
import jax
import jax.numpy as jnp
import numpy as np
from jax import lax
from jax.sharding import PartitionSpec as P

X_SIZE = 4
Z_SIZE = 16
CAPACITY = 5
Z_GROUPS = [[x * Z_SIZE + z for z in range(Z_SIZE)] for x in range(X_SIZE)]
X_GROUPS = [[x * Z_SIZE + z for x in range(X_SIZE)] for z in range(Z_SIZE)]


def silu_parts(gate_pre):
    sigmoid_val = jax.nn.sigmoid(gate_pre)
    return (gate_pre * sigmoid_val, sigmoid_val * (1.0 + gate_pre * (1.0 - sigmoid_val)))


def dequantize(values, scales):
    array_shape = values.shape
    blocked = values.astype(jnp.float32).reshape(
        array_shape[:-1] + (scales.shape[-1], array_shape[-1] // scales.shape[-1])
    )
    return (
        (blocked * scales.astype(jnp.float32)[..., None]).reshape(array_shape).astype(jnp.bfloat16)
    )


def route_tables(ids, counts, z_pos, tok_rows):
    count_float = counts.astype(jnp.float32)
    share = count_float / jnp.sum(count_float, axis=1, keepdims=True)
    experts = jnp.arange(X_SIZE, dtype=jnp.int32) * Z_SIZE + z_pos
    hit = ids[None] == experts[:, None, None]
    match = jnp.any(hit, axis=2)
    weight = jnp.sum(jnp.where(hit, share[None], 0.0), axis=2)
    ones = match.astype(jnp.bfloat16).reshape(X_SIZE * Z_SIZE, tok_rows)
    before = jnp.asarray(np.triu(np.ones((tok_rows, tok_rows)), 1), jnp.bfloat16)
    rank = jnp.dot(ones, before, preferred_element_type=jnp.float32).astype(jnp.int32)
    base = jnp.arange(Z_SIZE, dtype=jnp.int32)[None, :, None] * CAPACITY
    slot = (base + rank.reshape(X_SIZE, Z_SIZE, tok_rows)).reshape(X_SIZE, Z_SIZE * tok_rows)
    slot = jnp.where(match, slot, -1)
    lanes = jnp.arange(Z_SIZE * CAPACITY, dtype=jnp.int32)
    pick = slot[:, None, :] == lanes[None, :, None]
    slot_share = jnp.sum(jnp.where(pick, weight[:, None, :], 0.0), axis=2)
    pick = pick.reshape(X_SIZE * Z_SIZE * CAPACITY, Z_SIZE * tok_rows).astype(jnp.bfloat16)
    return (pick, slot_share.reshape(X_SIZE * Z_SIZE * CAPACITY))


def on_device(
    payload,
    block_scales,
    cotangent,
    expert_ids,
    route_counts,
    gate_up,
    down_weight,
    first_moment,
    second_moment,
):
    tok_rows, width = payload.shape
    replicas = lax.axis_size("rep")
    z_pos = lax.axis_index("exp") % Z_SIZE
    side = Z_SIZE * CAPACITY
    slot_count = X_SIZE * side
    activation = dequantize(payload, block_scales)
    routing = jnp.concatenate([expert_ids, route_counts], axis=1).astype(jnp.bfloat16)
    routing = jnp.pad(routing, ((0, 0), (0, 112)))
    act_all = lax.all_gather(
        jnp.concatenate([activation, routing], axis=1),
        "exp",
        axis=0,
        tiled=True,
        axis_index_groups=Z_GROUPS,
    )
    cot_all = lax.all_gather(cotangent, "exp", axis=0, tiled=True, axis_index_groups=Z_GROUPS)
    whole_gate_up = lax.all_gather(gate_up, "rep", axis=2, tiled=True)
    whole_down = lax.all_gather(down_weight, "rep", axis=2, tiled=True)
    top = expert_ids.shape[1]
    ids = act_all[:, width : width + top].astype(jnp.int32)
    counts = act_all[:, width + top : width + 2 * top].astype(jnp.int32)
    pick, slot_share = route_tables(ids, counts, z_pos, tok_rows)

    def to_experts(rows):
        return lax.all_to_all(
            rows.reshape(X_SIZE, side, width),
            "exp",
            split_axis=0,
            concat_axis=0,
            tiled=True,
            axis_index_groups=X_GROUPS,
        )

    act_rows = jnp.dot(pick, act_all[:, :width], preferred_element_type=jnp.float32)
    input_rows = to_experts(act_rows.astype(jnp.bfloat16)).reshape(slot_count, width)
    cot_rows = jnp.dot(pick, cot_all, preferred_element_type=jnp.float32)
    cot_rows = (slot_share[:, None] * cot_rows).astype(jnp.bfloat16)
    cotan_rows = to_experts(cot_rows).reshape(slot_count, width)
    pre_acts = jnp.einsum(
        "sd,tdf->tsf", input_rows, whole_gate_up[0], preferred_element_type=jnp.float32
    )
    hidden_grad = jnp.einsum(
        "sd,fd->sf", cotan_rows, whole_down[0], preferred_element_type=jnp.float32
    )
    silu_val, silu_slope = silu_parts(pre_acts[0])
    gate_grad = (hidden_grad * pre_acts[1] * silu_slope).astype(jnp.bfloat16)
    up_grad = (hidden_grad * silu_val).astype(jnp.bfloat16)
    row_grad = (
        jnp.einsum("sf,df->sd", gate_grad, whole_gate_up[0, 0], preferred_element_type=jnp.float32)
        + jnp.einsum("sf,df->sd", up_grad, whole_gate_up[0, 1], preferred_element_type=jnp.float32)
    ).astype(jnp.bfloat16)
    home = to_experts(row_grad).reshape(slot_count, width)
    partial = jnp.einsum("st,sd->td", pick, home, preferred_element_type=jnp.float32)
    d_activation = lax.psum_scatter(
        partial.astype(jnp.bfloat16),
        "exp",
        scatter_dimension=0,
        tiled=True,
        axis_index_groups=Z_GROUPS,
    )
    hidden_width = gate_grad.shape[1]
    both_grads = jnp.concatenate([gate_grad, up_grad], axis=1)
    term = jnp.einsum("sd,sf->df", input_rows, both_grads, preferred_element_type=jnp.float32)
    term = lax.optimization_barrier(term.astype(jnp.bfloat16))
    local_square = jnp.sum(jnp.square(term.astype(jnp.float32)))
    summed = lax.psum_scatter(term, "rep", scatter_dimension=0, tiled=True).astype(jnp.float32)
    shard_rows = width // replicas
    grad_shard = summed.reshape(shard_rows, 2, hidden_width).transpose(1, 0, 2)
    small_sum, big_sum = lax.psum((local_square, jnp.sum(jnp.square(grad_shard))), "rep")
    entry_count = 2.0 * width * hidden_width
    small_norm = small_sum / (replicas * entry_count)
    big_norm = big_sum / (replicas * replicas * entry_count)
    noise_gain = replicas * big_norm / (small_norm + 1e-06)
    new_first = 0.9 * first_moment + 0.1 * grad_shard[None]
    new_second = 0.95 * second_moment + 0.05 * jnp.square(grad_shard[None])
    weight_step = (noise_gain * new_first / (jnp.sqrt(new_second) + 1e-08)).astype(jnp.bfloat16)
    return (d_activation, new_first, new_second, weight_step)


def solution(mesh):
    tokens = P(("rep", "exp"), None)
    shards = P("exp", None, "rep", None)
    return jax.shard_map(
        on_device,
        mesh=mesh,
        in_specs=(tokens,) * 5 + (shards, P("exp", None, "rep"), shards, shards),
        out_specs=(tokens, shards, shards, shards),
        check_vma=False,
    )
```

profile of v0, /device:TPU:6, one launch (start us, length us, event | category | flops | bytes accessed | tf_op | source)
XLA Modules:
  0.0 364.9 jit_solution(17802854460447803655)
XLA Ops:
  7.2 0.0 copy-start.6
  7.2 0.0 all-gather.5.cloned.1.call-start
  7.2 0.8 copy.36
  8.0 0.8 copy.35
  8.8 0.8 copy.34
  9.5 0.1 fusion.26
  9.6 0.1 mul.102
  9.7 1.0 fusion.22
  10.7 0.7 pad_maximum_fusion
  11.4 0.0 all-gather.5.cloned.1.call-update
  11.4 0.0 all-gather.7.cloned.1.call-start
  11.5 0.7 all-gather.7.cloned.1.call-update
  12.2 0.0 all-gather.11.cloned.1.call-start
  12.2 0.7 all-gather.11.cloned.1.call-update
  12.9 0.0 all-gather.9.cloned.1.call-start
  13.0 0.5 all-gather.9.cloned.1.call-update
  13.5 0.1 eq.47
  13.6 0.1 add.68
  13.7 0.1 add.69
  13.8 75.3 %all-gather.5.cloned.1.call-done = bf16[512,2176]{1,0:T(8,128)(2,1)} async-done(((bf16[32,2176]{1,0:T(8,128)(2,1)}), bf16[512,2176]{1,0:T(8,128)(2,1)}) %all-gather.5.cloned.1.call-update) | async-done | bytes 2228240 | tf_op jit(solution)/shard_map/all_gather | solution.py:68
  89.0 1.1 fusion.30
  90.1 0.1 copy.42
  90.2 0.1 compare_reduce_fusion
  90.3 0.1 reshape.85
  90.4 0.0 copy-done.6
  90.4 0.2 convolution_convert_fusion.2
  90.6 0.1 copy.38
  90.7 0.1 reshape.86
  90.8 0.2 bitcast_compare_fusion
  91.0 3.5 convolution_convert_fusion.1
  94.5 4.8 %all-to-all-start.1 = ((bf16[4,80,2048]{2,1,0:T(8,128)(2,1)}), bf16[4,80,2048]{2,1,0:T(8,128)(2,1)S(1)}, u32[]{:S(2)}, u32[]{:S(2)}) async-start(bf16[4,80,2048]{2,1,0:T(8,128)(2,1)} %bitcast.4), calls=%async_computation.1 | async-start | bytes 2621440 | tf_op jit(solution)/shard_map/all_to_all | solution.py:84
  99.3 0.1 copy.43
  99.4 0.1 fusion.23
  99.5 0.2 select_reduce_fusion
  99.6 0.1 mul.107
  99.7 61.3 %all-gather.7.cloned.1.call-done = bf16[512,2048]{1,0:T(8,128)(2,1)} async-done(((bf16[32,2048]{1,0:T(8,128)(2,1)}), bf16[512,2048]{1,0:T(8,128)(2,1)}) %all-gather.7.cloned.1.call-update) | async-done | bytes 2097168 | tf_op jit(solution)/shard_map/all_gather | solution.py:75
  161.0 3.5 fusion.3
  164.5 0.0 all-to-all-done.1
  164.5 4.8 %all-to-all-start = ((bf16[4,80,2048]{2,1,0:T(8,128)(2,1)}), bf16[4,80,2048]{2,1,0:T(8,128)(2,1)S(1)}, u32[]{:S(2)}, u32[]{:S(2)}) async-start(bf16[4,80,2048]{2,1,0:T(8,128)(2,1)} %bitcast.1), calls=%async_computation | async-start | bytes 2621440 | tf_op jit(solution)/shard_map/all_to_all | solution.py:84
  169.3 0.0 reduce-scatter.5.cloned.1.call-start
  169.3 26.2 %all-gather.11.cloned.1.call-done = bf16[1,2,2048,384]{3,2,1,0:T(8,128)(2,1)} async-done(((bf16[1,2,256,384]{3,2,1,0:T(8,128)(2,1)}), bf16[1,2,2048,384]{3,2,1,0:T(8,128)(2,1)}) %all-gather.11.cloned.1.call-update) | async-done | bytes 3145744 | tf_op jit(solution)/shard_map/all_gather | solution.py:76
  195.5 4.0 %fusion.8 = f32[2,320,384]{2,1,0:T(8,128)} fusion(bf16[320,2048,1]{1,0,2:T(8,128)(2,1)S(1)} %bitcast.88, bf16[1,2,2048,384]{3,2,1,0:T(8,128)(2,1)} %all-gather.11.cloned.1.call-done), kind=kOutput, calls=%fused_computation.16 | convolution fusion | flops 1006632960 | bytes 5439488 | tf_op jit(solution)/shard_map/sd,tdf->tsf/dot_general | solution.py:98
  199.5 30.6 %all-gather.9.cloned.1.call-done = bf16[1,384,2048]{2,1,0:T(8,128)(2,1)} async-done(((bf16[1,384,256]{2,1,0:T(8,128)(2,1)}), bf16[1,384,2048]{2,1,0:T(8,128)(2,1)}) %all-gather.9.cloned.1.call-update) | async-done | bytes 1572880 | tf_op jit(solution)/shard_map/all_gather | solution.py:77
  230.1 0.0 all-to-all-done
  230.1 2.6 multiply_convert_fusion
  232.7 0.0 copy-start.4
  232.7 0.7 copy-done.4
  233.4 3.5 convolution_convert_fusion
  236.9 0.0 reduce-scatter.5.cloned.1.call-update
  236.9 0.0 reduce-scatter.3.cloned.1.call-start
  237.0 1.8 copy-done.1
  238.8 0.9 fusion.5
  239.7 0.1 copy-done.5
  239.7 0.9 fusion.2
  240.6 20.8 %all_to_all.15 = bf16[4,80,2048]{2,1,0:T(8,128)(2,1)S(1)} all-to-all(bf16[4,80,2048]{2,1,0:T(8,128)(2,1)S(1)} %bitcast.85), channel_id=1, replica_groups={{0,16,32,48},{1,17,33,49},{2,18,34,50},{3,19,35,51},{4,20,36,52},{5,21,..., dimensions={0} | all-to-all | bytes 2621440 | tf_op jit(solution)/shard_map/all_to_all | solution.py:84
  261.5 2.7 bitcast_convert_fusion
  264.1 0.0 reduce-scatter.3.cloned.1.call-update
  264.1 0.0 copy-done
  264.1 2.2 multiply_reduce_fusion
  266.4 15.5 %reduce-scatter.5.cloned.1.call-done = bf16[256,768]{1,0:T(8,128)(2,1)} async-done(((bf16[2048,768]{1,0:T(8,128)(2,1)}), bf16[256,768]{1,0:T(8,128)(2,1)}) %reduce-scatter.5.cloned.1.call-update) | async-done | bytes 393232 | tf_op jit(solution)/shard_map/reduce_scatter | solution.py:125
  281.8 1.8 convert_multiply_fusion.1
  283.6 13.5 %all-reduce.1 = (f32[]{:T(128)}, f32[]{:T(128)}) all-reduce(f32[]{:T(128)} %get-tuple-element.14, f32[]{:T(128)} %multiply_reduce_fusion), channel_id=1, replica_groups=mesh['rep'=8,'exp'=64] {'rep'}, use_global_device_ids=true, to_apply=%region_7.8 | all-reduce | flops 2 | bytes 16 | tf_op jit(solution)/shard_map/psum | solution.py:128
  298.5 1.4 divide_convert_fusion
  300.0 58.1 %reduce-scatter.3.cloned.1.call-done = bf16[32,2048]{1,0:T(8,128)(2,1)} async-done(((bf16[512,2048]{1,0:T(8,128)(2,1)}), bf16[32,2048]{1,0:T(8,128)(2,1)}) %reduce-scatter.3.cloned.1.call-update) | async-done | bytes 131088 | tf_op jit(solution)/shard_map/reduce_scatter | solution.py:113
  (16 shorter events, 0.1 us)
Async XLA Ops:
  7.2 83.3 %copy-start.6 = (bf16[32,32]{1,0:T(8,128)(2,1)S(1)}, bf16[32,32]{1,0:T(8,128)(2,1)}, u32[]{:S(2)}) copy-start(bf16[32,32]{1,0:T(8,128)(2,1)} %constant.52.clone) | copy-start | bytes 6148
  7.2 81.9 %all-gather.5.cloned.1.call-start = ((), (), s32[]{:S(2)}) async-start(), calls=%async_computation.5 | async-start | bytes 2367488 | tf_op jit(solution)/shard_map/all_gather | solution.py:68
  11.4 149.6 %all-gather.7.cloned.1.call-start = ((), (), s32[]{:S(2)}) async-start(), calls=%async_computation.6 | async-start | bytes 2228224 | tf_op jit(solution)/shard_map/all_gather | solution.py:75
  12.2 183.3 %all-gather.11.cloned.1.call-start = ((), (), s32[]{:S(2)}) async-start(), calls=%async_computation.8 | async-start | bytes 3538944 | tf_op jit(solution)/shard_map/all_gather | solution.py:76
  12.9 217.2 %all-gather.9.cloned.1.call-start = ((), (), s32[]{:S(2)}) async-start(), calls=%async_computation.7 | async-start | bytes 1769472 | tf_op jit(solution)/shard_map/all_gather | solution.py:77
  94.5 70.1 %all-to-all-start.1 = ((bf16[4,80,2048]{2,1,0:T(8,128)(2,1)}), bf16[4,80,2048]{2,1,0:T(8,128)(2,1)S(1)}, u32[]{:S(2)}, u32[]{:S(2)}) async-start(bf16[4,80,2048]{2,1,0:T(8,128)(2,1)} %bitcast.4), calls=%async_computation.1 | async-start | bytes 2621440 | tf_op jit(solution)/shard_map/all_to_all | solution.py:84
  164.5 65.6 %all-to-all-start = ((bf16[4,80,2048]{2,1,0:T(8,128)(2,1)}), bf16[4,80,2048]{2,1,0:T(8,128)(2,1)S(1)}, u32[]{:S(2)}, u32[]{:S(2)}) async-start(bf16[4,80,2048]{2,1,0:T(8,128)(2,1)} %bitcast.1), calls=%async_computation | async-start | bytes 2621440 | tf_op jit(solution)/shard_map/all_to_all | solution.py:84
  169.3 112.5 %reduce-scatter.5.cloned.1.call-start = ((), (), s32[]{:S(2)}) async-start(), calls=%async_computation.10 | async-start | bytes 3538944 | tf_op jit(solution)/shard_map/reduce_scatter | solution.py:125
  232.7 0.7 copy-start.4
  236.9 1.9 copy-start.1
  236.9 121.2 %reduce-scatter.3.cloned.1.call-start = ((), (), s32[]{:S(2)}) async-start(), calls=%async_computation.9 | async-start | bytes 2228224 | tf_op jit(solution)/shard_map/reduce_scatter | solution.py:113
  238.8 0.9 copy-start.5
  261.5 2.7 copy-start
  266.4 32.1 %copy-start.2 = (f32[1,2,256,384]{3,2,1,0:T(8,128)S(1)}, f32[1,2,256,384]{3,2,1,0:T(8,128)}, u32[]{:S(2)}) copy-start(f32[1,2,256,384]{3,2,1,0:T(8,128)} %param.18) | copy-start | bytes 2359300
  266.4 32.1 %copy-start.3 = (f32[1,2,256,384]{3,2,1,0:T(8,128)S(1)}, f32[1,2,256,384]{3,2,1,0:T(8,128)}, u32[]{:S(2)}) copy-start(f32[1,2,256,384]{3,2,1,0:T(8,128)} %param.17) | copy-start | bytes 2359300
Sparse Core Ops, SparseCore 0:
  11.6 77.4 all-gather.4
  91.1 69.8 all-gather.6
  163.2 32.2 all-gather.10
  197.4 32.5 all-gather.8
  237.0 44.7 reduce-scatter.4
  285.1 72.9 reduce-scatter.2
where the time goes:
time: 366 us; the launch traced here: 365 us
  waiting for transfers between devices  269 us (73%)
  blocking collectives  34.4 us (9%)
  matrix products  21.7 us (6%)
  between operations  15.6 us (4%)
  starting transfers between devices  9.77 us (3%)
  other arithmetic  7.83 us (2%)
  local copies, waits for them, and re-layouts  6.8 us (2%)
    all_gather x1, waiting for transfers between devices, on_device(): lax.all_gather(jnp.concatenate([activation, routing], axis=1), 'exp', axi...  75.3 us
    all_gather x1, waiting for transfers between devices, on_device(): lax.all_gather(cotangent, 'exp', axis=0, tiled=True, axis_index_groups=Z_...  61.3 us
    reduce_scatter x1, waiting for transfers between devices, on_device(): lax.psum_scatter(partial.astype(jnp.bfloat16), 'exp', scatter_dimension=0...  58.1 us
    all_gather x1, waiting for transfers between devices, on_device(): whole_down = lax.all_gather(down_weight, 'rep', axis=2, tiled=True)  30.6 us
    all_gather x1, waiting for transfers between devices, on_device(): whole_gate_up = lax.all_gather(gate_up, 'rep', axis=2, tiled=True)  26.2 us
    all_to_all x1, blocking collectives, to_experts(): lax.all_to_all(rows.reshape(X_SIZE, side, width), 'exp', split_axis=0, co...  20.8 us
    reduce_scatter x1, waiting for transfers between devices, on_device(): lax.psum_scatter(term, 'rep', scatter_dimension=0, tiled=True)  15.5 us
    psum x1, blocking collectives, on_device(): lax.psum((local_square, jnp.sum(jnp.square(grad_shard))), 'rep')  13.5 us
  transfers between devices with their start and end apart: 8, of which 6 were waited for; matrix products, arithmetic and copies ran while one was open for 6% of the time, Pallas kernels for 0%

commit v1 on v0

--- a/solution.py
+++ b/solution.py
@@ -74,7 +74,16 @@
     )
     cot_all = lax.all_gather(cotangent, "exp", axis=0, tiled=True, axis_index_groups=Z_GROUPS)
     whole_gate_up = lax.all_gather(gate_up, "rep", axis=2, tiled=True)
-    whole_down = lax.all_gather(down_weight, "rep", axis=2, tiled=True)
+    ways = lax.axis_size("rep")
+    up = [(d, (d + 1) % ways) for d in range(ways)]
+    down = [(d, (d - 1) % ways) for d in range(ways)]
+    earlier, later = ([down_weight], [down_weight])
+    for _ in range(ways // 2):
+        earlier.append(lax.ppermute(earlier[-1], "rep", up))
+    for _ in range((ways - 1) // 2):
+        later.append(lax.ppermute(later[-1], "rep", down))
+    line = jnp.concatenate([*earlier[::-1], *later[1:]], axis=2)
+    whole_down = jnp.roll(line, (lax.axis_index("rep") - ways // 2) * down_weight.shape[2], axis=2)
     top = expert_ids.shape[1]
     ids = act_all[:, width : width + top].astype(jnp.int32)
     counts = act_all[:, width + top : width + 2 * top].astype(jnp.int32)

time: 366 us -> 334 us (0.913)
  waiting for transfers between devices: 269 us -> 214 us
  local copies, waits for them, and re-layouts: 6.8 us -> 19.3 us
  starting transfers between devices: 9.77 us -> 18.6 us
    all_gather x1, waiting for transfers between devices: 75.3 us -> 43.5 us  [on_device(): lax.all_gather(jnp.concatenate([activation, routing], axis=1), 'exp', axi...]
    all_gather x1 -> x0, waiting for transfers between devices: 30.6 us -> none  [on_device(): whole_down = lax.all_gather(down_weight, 'rep', axis=2, tiled=True)]
    ppermute x0 -> x7, waiting for transfers between devices: none -> 16.2 us  [the longest x4 16.1 us: on_device(): earlier.append(lax.ppermute(earlier[-1], 'rep', up))]
    unnamed x18 -> x33, local copies, waits for them, and re-layouts: 4.26 us -> 15.1 us
    ppermute x0 -> x7, starting transfers between devices: none -> 8.99 us  [the longest x3 8.96 us: on_device(): later.append(lax.ppermute(later[-1], 'rep', down))]
    all_gather x1, waiting for transfers between devices: 26.2 us -> 21.6 us  [on_device(): whole_gate_up = lax.all_gather(gate_up, 'rep', axis=2, tiled=True)]
  transfers between devices with their start and end apart: 8 -> 14, of which waited for: 6 -> 10; matrix products, arithmetic and copies ran while one was open for 6% -> 11% of each run, Pallas kernels for 0% -> 0%
where the time goes in v1:
time: 334 us; the launch traced here: 333 us
  waiting for transfers between devices  214 us (64%)
  blocking collectives  34.3 us (10%)
  matrix products  21.8 us (7%)
  local copies, waits for them, and re-layouts  19.3 us (6%)
  starting transfers between devices  18.6 us (6%)
  between operations  15.3 us (5%)
  other arithmetic  9.21 us (3%)
    all_gather x1, waiting for transfers between devices, on_device(): lax.all_gather(cotangent, 'exp', axis=0, tiled=True, axis_index_groups=Z_...  60.6 us
    reduce_scatter x1, waiting for transfers between devices, on_device(): lax.psum_scatter(partial.astype(jnp.bfloat16), 'exp', scatter_dimension=0...  56.4 us
    all_gather x1, waiting for transfers between devices, on_device(): lax.all_gather(jnp.concatenate([activation, routing], axis=1), 'exp', axi...  43.5 us
    all_gather x1, waiting for transfers between devices, on_device(): whole_gate_up = lax.all_gather(gate_up, 'rep', axis=2, tiled=True)  21.6 us
    all_to_all x1, blocking collectives, to_experts(): lax.all_to_all(rows.reshape(X_SIZE, side, width), 'exp', split_axis=0, co...  20.8 us
    ppermute x4, waiting for transfers between devices, on_device(): earlier.append(lax.ppermute(earlier[-1], 'rep', up))  16.1 us
    unnamed x33, local copies, waits for them, and re-layouts  15.1 us
    reduce_scatter x1, waiting for transfers between devices, on_device(): lax.psum_scatter(term, 'rep', scatter_dimension=0, tiled=True)  14.6 us
  transfers between devices with their start and end apart: 14, of which 10 were waited for; matrix products, arithmetic and copies ran while one was open for 11% of the time, Pallas kernels for 0%

profile of v1, /device:TPU:6, one launch (start us, length us, event | category | flops | bytes accessed | tf_op | source)
XLA Modules:
  0.0 332.8 jit_solution(4770232278290792577)
XLA Ops:
  7.2 0.8 copy.34
  8.0 0.8 copy.35
  8.8 0.8 copy.36
  9.6 0.1 mul.105
  9.8 1.0 fusion.23
  10.8 0.7 pad_maximum_fusion
  11.5 0.7 all-gather.6.cloned.1.call-update
  12.3 0.7 all-gather.8.cloned.1.call-update
  13.0 6.5 %collective-permute-done = bf16[1,384,256]{2,1,0:T(8,128)(2,1)S(1)} collective-permute-done((bf16[1,384,256]{2,1,0:T(8,128)(2,1)}, bf16[1,384,256]{2,1,0:T(8,128)(2,1)S(1)}, u32[]{:S(2)}, u32[]{:S(2)}) %collective-permute-start) | collective-permute-done | bytes 196640 | tf_op jit(solution)/shard_map/ppermute | solution.py:82
  19.5 3.0 collective-permute-start.4
  22.5 3.3 %collective-permute-done.1 = bf16[1,384,256]{2,1,0:T(8,128)(2,1)S(1)} collective-permute-done((bf16[1,384,256]{2,1,0:T(8,128)(2,1)S(1)}, bf16[1,384,256]{2,1,0:T(8,128)(2,1)S(1)}, u32[]{:S(2)}, u32[]{:S(2)}) %collective-permute-start.1) | collective-permute-done | bytes 196640 | tf_op jit(solution)/shard_map/ppermute | solution.py:82
  25.8 0.1 eq.50
  26.0 3.0 collective-permute-start.5
  29.0 3.1 collective-permute-done.2
  32.3 3.0 collective-permute-start.6
  35.3 3.1 collective-permute-done.3
  38.4 0.7 constant_dynamic-update-slice_fusion.15
  39.1 0.7 constant_dynamic-update-slice_fusion.14
  39.9 0.7 constant_dynamic-update-slice_fusion.13
  40.6 0.7 constant_dynamic-update-slice_fusion.12
  41.3 0.7 constant_dynamic-update-slice_fusion.11
  42.0 0.7 constant_dynamic-update-slice_fusion.10
  42.8 0.7 constant_dynamic-update-slice_fusion.9
  43.5 0.7 constant_dynamic-update-slice_fusion.8
  44.2 0.7 constant_dynamic-update-slice_fusion.7
  44.9 0.7 constant_dynamic-update-slice_fusion.6
  45.6 43.5 %all-gather.4.cloned.1.call-done = bf16[512,2176]{1,0:T(8,128)(2,1)} async-done(((bf16[32,2176]{1,0:T(8,128)(2,1)}), bf16[512,2176]{1,0:T(8,128)(2,1)}) %all-gather.4.cloned.1.call-update) | async-done | bytes 2228240 | tf_op jit(solution)/shard_map/all_gather | solution.py:68
  89.1 1.1 fusion.32
  90.3 0.1 compare_reduce_fusion
  90.4 0.1 reshape.85
  90.5 0.2 convolution_convert_fusion.2
  90.6 0.1 copy.38
  90.7 0.1 reshape.86
  90.8 0.2 bitcast_compare_fusion
  91.0 3.5 %convolution_convert_fusion.1 = bf16[320,2048]{1,0:T(8,128)(2,1)} fusion(pred[320,512]{1,0:T(32,128)(4,1)S(1)} %bitcast_compare_fusion, bf16[512,2176]{1,0:T(8,128)(2,1)} %all-gather.4.cloned.1.call-done), kind=kOutput, calls=%fused_computation.9 | convolution fusion | flops 671744000 | bytes 3571712 | tf_op jit(solution)/shard_map/dot_general | solution.py:102
  94.5 4.7 %all-to-all-start.1 = ((bf16[4,80,2048]{2,1,0:T(8,128)(2,1)}), bf16[4,80,2048]{2,1,0:T(8,128)(2,1)S(1)}, u32[]{:S(2)}, u32[]{:S(2)}) async-start(bf16[4,80,2048]{2,1,0:T(8,128)(2,1)} %bitcast.4), calls=%async_computation.1 | async-start | bytes 2621440 | tf_op jit(solution)/shard_map/all_to_all | solution.py:93
  99.2 0.7 constant_dynamic-update-slice_fusion.5
  100.0 0.1 fusion.24
  100.1 0.2 select_reduce_fusion
  100.3 0.1 mul.110
  100.4 60.6 %all-gather.6.cloned.1.call-done = bf16[512,2048]{1,0:T(8,128)(2,1)} async-done(((bf16[32,2048]{1,0:T(8,128)(2,1)}), bf16[512,2048]{1,0:T(8,128)(2,1)}) %all-gather.6.cloned.1.call-update) | async-done | bytes 2097168 | tf_op jit(solution)/shard_map/all_gather | solution.py:75
  161.0 3.5 %fusion.3 = bf16[320,2048]{1,0:T(8,128)(2,1)} fusion(pred[320,512]{1,0:T(32,128)(4,1)S(1)} %bitcast_compare_fusion, bf16[512,2048]{1,0:T(8,128)(2,1)} %all-gather.6.cloned.1.call-done, f32[320]{0:T(512)S(1)} %mul.110), kind=kOutput, calls=%fused_computation.8 | convolution fusion | flops 672399360 | bytes 3572992 | tf_op jit(solution)/shard_map/dot_general | solution.py:104
  164.5 4.8 %all-to-all-start = ((bf16[4,80,2048]{2,1,0:T(8,128)(2,1)}), bf16[4,80,2048]{2,1,0:T(8,128)(2,1)S(1)}, u32[]{:S(2)}, u32[]{:S(2)}) async-start(bf16[4,80,2048]{2,1,0:T(8,128)(2,1)} %bitcast.1), calls=%async_computation | async-start | bytes 2621440 | tf_op jit(solution)/shard_map/all_to_all | solution.py:93
  169.3 0.7 constant_dynamic-update-slice_fusion.4
  170.0 0.8 constant_dynamic-update-slice_fusion.3
  170.8 0.7 constant_dynamic-update-slice_fusion.2
  171.5 0.7 constant_dynamic-update-slice_fusion.1
  172.2 1.6 constant_dynamic-update-slice_fusion
  173.9 21.6 %all-gather.8.cloned.1.call-done = bf16[1,2,2048,384]{3,2,1,0:T(8,128)(2,1)} async-done(((bf16[1,2,256,384]{3,2,1,0:T(8,128)(2,1)}), bf16[1,2,2048,384]{3,2,1,0:T(8,128)(2,1)}) %all-gather.8.cloned.1.call-update) | async-done | bytes 3145744 | tf_op jit(solution)/shard_map/all_gather | solution.py:76
  195.4 4.1 %fusion.9 = f32[2,320,384]{2,1,0:T(8,128)} fusion(bf16[320,2048,1]{1,0,2:T(8,128)(2,1)S(1)} %bitcast.88, bf16[1,2,2048,384]{3,2,1,0:T(8,128)(2,1)} %all-gather.8.cloned.1.call-done), kind=kOutput, calls=%fused_computation.17 | convolution fusion | flops 1006632960 | bytes 5439488 | tf_op jit(solution)/shard_map/sd,tdf->tsf/dot_general | solution.py:107
  199.6 2.6 multiply_convert_fusion
  202.1 0.7 copy-done.4
  202.8 3.5 %convolution_convert_fusion = bf16[2048,768]{1,0:T(8,128)(2,1)} fusion(bf16[320,2048]{1,0:T(8,128)(2,1)S(1)} %bitcast.89, bf16[320,384]{1,0:T(8,128)(2,1)S(1)} %get-tuple-element.11, bf16[320,384]{1,0:T(8,128)(2,1)S(1)} %get-tuple-element.12), kind=kOutput, calls=%fused_computation.2 | convolution fusion | flops 1009188864 | bytes 4947968 | tf_op jit(solution)/shard_map/sd,sf->df/dot_general | solution.py:131
  206.4 1.8 copy-done.1
  208.2 0.9 fusion.5
  209.2 0.9 fusion.2
  210.1 20.8 %all_to_all.15 = bf16[4,80,2048]{2,1,0:T(8,128)(2,1)S(1)} all-to-all(bf16[4,80,2048]{2,1,0:T(8,128)(2,1)S(1)} %bitcast.85), channel_id=1, replica_groups={{0,16,32,48},{1,17,33,49},{2,18,34,50},{3,19,35,51},{4,20,36,52},{5,21,..., dimensions={0} | all-to-all | bytes 2621440 | tf_op jit(solution)/shard_map/all_to_all | solution.py:93
  230.9 2.6 bitcast_convert_fusion
  233.6 2.2 multiply_reduce_fusion
  235.8 14.6 %reduce-scatter.5.cloned.1.call-done = bf16[256,768]{1,0:T(8,128)(2,1)} async-done(((bf16[2048,768]{1,0:T(8,128)(2,1)}), bf16[256,768]{1,0:T(8,128)(2,1)}) %reduce-scatter.5.cloned.1.call-update) | async-done | bytes 393232 | tf_op jit(solution)/shard_map/reduce_scatter | solution.py:134
  250.4 1.8 convert_multiply_fusion.1
  252.2 13.5 %all-reduce.1 = (f32[]{:T(128)}, f32[]{:T(128)}) all-reduce(f32[]{:T(128)} %get-tuple-element.14, f32[]{:T(128)} %multiply_reduce_fusion), channel_id=1, replica_groups=mesh['rep'=8,'exp'=64] {'rep'}, use_global_device_ids=true, to_apply=%region_7.8 | all-reduce | flops 2 | bytes 16 | tf_op jit(solution)/shard_map/psum | solution.py:137
  267.0 2.8 divide_convert_fusion
  269.8 56.4 %reduce-scatter.3.cloned.1.call-done = bf16[32,2048]{1,0:T(8,128)(2,1)} async-done(((bf16[512,2048]{1,0:T(8,128)(2,1)}), bf16[32,2048]{1,0:T(8,128)(2,1)}) %reduce-scatter.3.cloned.1.call-update) | async-done | bytes 131088 | tf_op jit(solution)/shard_map/reduce_scatter | solution.py:122
  (43 shorter events, 0.9 us)
Async XLA Ops:
  7.2 34.2 %copy-start.2 = (bf16[1,384,256]{2,1,0:T(8,128)(2,1)S(1)}, bf16[1,384,256]{2,1,0:T(8,128)(2,1)}, u32[]{:S(2)}) copy-start(bf16[1,384,256]{2,1,0:T(8,128)(2,1)} %param.16) | copy-start | bytes 589828
  7.2 81.9 %all-gather.4.cloned.1.call-start = ((), (), s32[]{:S(2)}) async-start(), calls=%async_computation.5 | async-start | bytes 2367488 | tf_op jit(solution)/shard_map/all_gather | solution.py:68
  9.8 80.7 %copy-start.6 = (bf16[32,32]{1,0:T(8,128)(2,1)S(1)}, bf16[32,32]{1,0:T(8,128)(2,1)}, u32[]{:S(2)}) copy-start(bf16[32,32]{1,0:T(8,128)(2,1)} %constant.83.clone) | copy-start | bytes 6148
  11.5 149.5 %all-gather.6.cloned.1.call-start = ((), (), s32[]{:S(2)}) async-start(), calls=%async_computation.6 | async-start | bytes 2228224 | tf_op jit(solution)/shard_map/all_gather | solution.py:75
  12.2 183.2 %all-gather.8.cloned.1.call-start = ((), (), s32[]{:S(2)}) async-start(), calls=%async_computation.7 | async-start | bytes 3538944 | tf_op jit(solution)/shard_map/all_gather | solution.py:76
  13.0 6.5 %collective-permute-start = (bf16[1,384,256]{2,1,0:T(8,128)(2,1)}, bf16[1,384,256]{2,1,0:T(8,128)(2,1)S(1)}, u32[]{:S(2)}, u32[]{:S(2)}) collective-permute-start(bf16[1,384,256]{2,1,0:T(8,128)(2,1)} %param.16), channel_id=1, source_target_pairs={{0,64},{64,128},{128,192},{192,256},{256,320},{320,384},{384,448},... | collective-permute-start | bytes 589832 | tf_op jit(solution)/shard_map/ppermute | solution.py:82
  19.5 6.3 %collective-permute-start.1 = (bf16[1,384,256]{2,1,0:T(8,128)(2,1)S(1)}, bf16[1,384,256]{2,1,0:T(8,128)(2,1)S(1)}, u32[]{:S(2)}, u32[]{:S(2)}) collective-permute-start(bf16[1,384,256]{2,1,0:T(8,128)(2,1)S(1)} %collective-permute-done), channel_id=1, source_target_pairs={{0,64},{64,128},{128,192},{192,256},{256,320},{320,384},{384,448},... | collective-permute-start | bytes 589832 | tf_op jit(solution)/shard_map/ppermute | solution.py:82
  19.5 6.5 %collective-permute-start.4 = (bf16[1,384,256]{2,1,0:T(8,128)(2,1)}, bf16[1,384,256]{2,1,0:T(8,128)(2,1)S(1)}, u32[]{:S(2)}, u32[]{:S(2)}) collective-permute-start(bf16[1,384,256]{2,1,0:T(8,128)(2,1)} %param.16), channel_id=1, source_target_pairs={{0,448},{64,0},{128,64},{192,128},{256,192},{320,256},{384,320},{4... | collective-permute-start | bytes 589832 | tf_op jit(solution)/shard_map/ppermute | solution.py:84
  25.8 6.3 %collective-permute-start.2 = (bf16[1,384,256]{2,1,0:T(8,128)(2,1)S(1)}, bf16[1,384,256]{2,1,0:T(8,128)(2,1)S(1)}, u32[]{:S(2)}, u32[]{:S(2)}) collective-permute-start(bf16[1,384,256]{2,1,0:T(8,128)(2,1)S(1)} %collective-permute-done.1), channel_id=1, source_target_pairs={{0,64},{64,128},{128,192},{192,256},{256,320},{320,384},{384,448},... | collective-permute-start | bytes 589832 | tf_op jit(solution)/shard_map/ppermute | solution.py:82
  26.0 6.3 %collective-permute-start.5 = (bf16[1,384,256]{2,1,0:T(8,128)(2,1)S(1)}, bf16[1,384,256]{2,1,0:T(8,128)(2,1)S(1)}, u32[]{:S(2)}, u32[]{:S(2)}) collective-permute-start(bf16[1,384,256]{2,1,0:T(8,128)(2,1)S(1)} %collective-permute-done.4), channel_id=1, source_target_pairs={{0,448},{64,0},{128,64},{192,128},{256,192},{320,256},{384,320},{4... | collective-permute-start | bytes 589832 | tf_op jit(solution)/shard_map/ppermute | solution.py:84
  32.1 6.3 %collective-permute-start.3 = (bf16[1,384,256]{2,1,0:T(8,128)(2,1)S(1)}, bf16[1,384,256]{2,1,0:T(8,128)(2,1)S(1)}, u32[]{:S(2)}, u32[]{:S(2)}) collective-permute-start(bf16[1,384,256]{2,1,0:T(8,128)(2,1)S(1)} %collective-permute-done.2), channel_id=1, source_target_pairs={{0,64},{64,128},{128,192},{192,256},{256,320},{320,384},{384,448},... | collective-permute-start | bytes 589832 | tf_op jit(solution)/shard_map/ppermute | solution.py:82
  32.3 11.2 %collective-permute-start.6 = (bf16[1,384,256]{2,1,0:T(8,128)(2,1)S(1)}, bf16[1,384,256]{2,1,0:T(8,128)(2,1)S(1)}, u32[]{:S(2)}, u32[]{:S(2)}) collective-permute-start(bf16[1,384,256]{2,1,0:T(8,128)(2,1)S(1)} %collective-permute-done.5), channel_id=1, source_target_pairs={{0,448},{64,0},{128,64},{192,128},{256,192},{320,256},{384,320},{4... | collective-permute-start | bytes 589832 | tf_op jit(solution)/shard_map/ppermute | solution.py:84
  43.5 121.0 %copy-start.3 = (bf16[1,384,256]{2,1,0:T(8,128)(2,1)}, bf16[1,384,256]{2,1,0:T(8,128)(2,1)S(1)}, u32[]{:S(2)}) copy-start(bf16[1,384,256]{2,1,0:T(8,128)(2,1)S(1)} %collective-permute-done.6) | copy-start | bytes 589828
  94.5 70.0 %all-to-all-start.1 = ((bf16[4,80,2048]{2,1,0:T(8,128)(2,1)}), bf16[4,80,2048]{2,1,0:T(8,128)(2,1)S(1)}, u32[]{:S(2)}, u32[]{:S(2)}) async-start(bf16[4,80,2048]{2,1,0:T(8,128)(2,1)} %bitcast.4), calls=%async_computation.1 | async-start | bytes 2621440 | tf_op jit(solution)/shard_map/all_to_all | solution.py:93
  164.5 35.0 %all-to-all-start = ((bf16[4,80,2048]{2,1,0:T(8,128)(2,1)}), bf16[4,80,2048]{2,1,0:T(8,128)(2,1)S(1)}, u32[]{:S(2)}, u32[]{:S(2)}) async-start(bf16[4,80,2048]{2,1,0:T(8,128)(2,1)} %bitcast.1), calls=%async_computation | async-start | bytes 2621440 | tf_op jit(solution)/shard_map/all_to_all | solution.py:93
  169.3 81.1 %reduce-scatter.5.cloned.1.call-start = ((), (), s32[]{:S(2)}) async-start(), calls=%async_computation.9 | async-start | bytes 3538944 | tf_op jit(solution)/shard_map/reduce_scatter | solution.py:134
  202.1 0.7 copy-start.4
  206.3 1.9 copy-start.1
  206.4 119.9 %reduce-scatter.3.cloned.1.call-start = ((), (), s32[]{:S(2)}) async-start(), calls=%async_computation.8 | async-start | bytes 2228224 | tf_op jit(solution)/shard_map/reduce_scatter | solution.py:122
  208.2 0.9 copy-start.5
  230.9 2.7 copy-start
Sparse Core Ops, SparseCore 0:
  11.6 77.4 all-gather.3
  91.2 69.7 all-gather.5
  163.1 32.2 all-gather.7
  206.5 43.8 reduce-scatter.4
  253.6 72.5 reduce-scatter.2
